TPU v7x, 512 devices: a whole 4x4x16 slice. The times are simulated.
512 devices in a mesh: req: 64 (over y, z), head: 8 (over x, core).
Axes of the slice: x: 4, y: 4, z: 16, core: 2. Of those that a mesh axis runs over, the one named last changes fastest.
Arguments:
- tokens: bfloat16 [256, 2048], P('req'), may hold values from -1.1953125 to 1.1953125
- lengths: int32 [256], replicated, may hold values from 1 to 1021, as said below
- kv_cache: bfloat16 [1, 2, 65536, 8, 128], P(None, None, 'req', 'head'), may hold values from -24 to 24
- w_qkv: bfloat16 [1, 2048, 8, 512], P(None, 'req', 'head'), may hold values from -0.125 to 0.125
- w_headgate: bfloat16 [1, 2048, 16], P(None, None, 'head'), may hold values from -0.125 to 0.125
- w_out: bfloat16 [1, 2048, 2048], P(None, 'head', 'req'), may hold values from -0.5 to 0.5
- in_gain: float32 [1, 2048], replicated, may hold values from 0.5 to 1.5
- q_gain: float32 [1, 128], replicated, may hold values from 0.1 to 1.9
- k_gain: float32 [1, 128], replicated, may hold values from 0.1 to 1.9
- post_gain: float32 [1, 2048], replicated, may hold values from 0.5 to 1.5
- w_gate: bfloat16 [1, 2048, 6144], P(None, 'head', 'req'), may hold values from -0.125 to 0.125
- w_up: bfloat16 [1, 2048, 6144], P(None, 'head', 'req'), may hold values from -0.125 to 0.125
- w_down: bfloat16 [1, 6144, 2048], P(None, 'req', 'head'), may hold values from -0.078125 to 0.078125
- final_gain: float32 [2048], replicated, may hold values from 0.5 to 1.5
- w_vocab: bfloat16 [2048, 131072], P(None, ('req', 'head')), may hold values from -0.125 to 0.125
Outputs:
- logits: bfloat16 [256, 131072], P(None, ('req', 'head'))
Inputs may be any that keep to these rules, and one draw needn't show every extreme that they name: On every index of req the lengths of its 4 requests sum to at most 1024. On 8 indices, drawn anew, they sum to exactly 1024 and one request there is longer than 512; on one of these the other requests hold one token each. On every other index each length is at most 128 and one is exactly 128.
All inputs are finite; a program needn't handle non-finite values.
Results may differ from a plain program's by a relative error of at most 0.015.
Values may be sent and summed in bfloat16 or wider, within the bound.
No kernel may reach another device: no remote copies, remote signals or barrier semaphores. Data moves between devices by JAX's collectives and lax.ppermute only.
A program may use at most 64 MiB of HBM per device.

v0:
```python
import jax
import jax.numpy as jnp
from jax import lax
from jax.sharding import Mesh
from jax.sharding import PartitionSpec as P

EPSILON = 1e-06
ROPE_THETA = 1000000.0
Y, Z, X, C = (4, 16, 4, 2)
F32, BF16 = (jnp.float32, jnp.bfloat16)


def rms_scale(values, gain):
    mean_square = jnp.mean(values * values, axis=-1, keepdims=True)
    return values * lax.rsqrt(mean_square + EPSILON) * gain


def rotate(values, cosine, sine):
    half = values.shape[-1] // 2
    a, b = (values[..., :half], values[..., half:])
    return jnp.concatenate([a * cosine - b * sine, b * cosine + a * sine], axis=-1)


def swap(values, axes):
    return lax.all_to_all(values, axes, split_axis=0, concat_axis=0, tiled=True)


def spread(values, axes, count):
    return swap(jnp.broadcast_to(values[None], (count,) + values.shape), axes)


def local(
    tokens,
    lengths,
    kv_cache,
    w_qkv,
    w_headgate,
    w_out,
    in_gain,
    q_gain,
    k_gain,
    post_gain,
    w_gate,
    w_up,
    w_down,
    final_gain,
    w_vocab,
):
    rows, width = tokens.shape
    head_dim = q_gain.shape[1]
    columns = w_qkv.shape[3]
    req = lax.axis_index(("y", "z"))
    ix, ic = (lax.axis_index("x"), lax.axis_index("c"))
    qkv_block = lax.all_gather(w_qkv[0, :, 0], "y", axis=0, tiled=True)
    out_part = lax.all_gather(w_out[0].T, "z", axis=0, tiled=True)
    out_block = lax.all_gather(out_part, "y", axis=0, tiled=True)
    gate_up = jnp.concatenate([w_gate[0].T, w_up[0].T], axis=0)
    gate_up = lax.all_gather(gate_up, "x", axis=0)
    down = lax.all_gather(w_down[0], "x", axis=0)
    positions = lax.dynamic_slice_in_dim(lengths, req * rows, rows)
    starts = jnp.cumsum(positions) - positions
    limits = starts + positions
    normed = rms_scale(tokens.astype(F32), in_gain[0]).astype(BF16)
    head_gate = jax.nn.sigmoid(jnp.dot(normed, w_headgate[0], preferred_element_type=F32))
    depth = width // (Y * Z)
    sent = normed.reshape(rows, Y, Z, depth).transpose(2, 0, 1, 3).reshape(Z, rows, Y * depth)
    arrived = swap(sent, "z").reshape(Z * rows, Y * depth)
    part = jnp.dot(arrived, qkv_block, preferred_element_type=F32).astype(BF16)
    qkv = jnp.sum(swap(part.reshape(Z, rows, columns), "z").astype(F32), axis=0)
    half = head_dim // 2
    frequency = ROPE_THETA ** (-2.0 * jnp.arange(half, dtype=F32) / head_dim)
    angles = positions.astype(F32)[:, None] * frequency[None, :]
    cosine, sine = (jnp.cos(angles), jnp.sin(angles))
    query = qkv[:, : 2 * head_dim].reshape(rows, 2, head_dim)
    query = rotate(rms_scale(query, q_gain[0]), cosine[:, None], sine[:, None]).astype(BF16)
    key = qkv[:, 2 * head_dim : 3 * head_dim]
    key = rotate(rms_scale(key, k_gain[0]), cosine, sine).astype(BF16)
    value = qkv[:, 3 * head_dim :].astype(BF16)
    scale = head_dim ** (-0.5)
    keys, values = (kv_cache[0, 0, :, 0], kv_cache[0, 1, :, 0])
    slots = keys.shape[0]
    score = jnp.einsum("rqd,sd->rqs", query, keys, preferred_element_type=F32) * scale
    slot = jnp.arange(slots, dtype=jnp.int32)
    inside = (slot[None, :] >= starts[:, None]) & (slot[None, :] < limits[:, None])
    weight = jnp.where(inside[:, None, :], jnp.exp(score), 0.0)
    own = jnp.exp(jnp.sum(query.astype(F32) * key.astype(F32)[:, None], axis=-1) * scale)
    total = jnp.sum(weight, axis=-1) + own
    summed = jnp.einsum("rqs,sd->rqd", weight.astype(BF16), values, preferred_element_type=F32)
    summed = summed + own.astype(BF16).astype(F32)[..., None] * value.astype(F32)[:, None]
    attended = summed / total[..., None]
    mixed = (attended * head_gate[..., None]).astype(BF16).reshape(rows, 2 * head_dim)
    part = lax.dot_general(mixed, out_block, (((1,), (1,)), ((), ())), preferred_element_type=F32)
    projected = jnp.sum(spread(part, ("x", "c"), X * C), axis=0)
    stream = (tokens.astype(F32) + projected).astype(BF16)
    normed_two = rms_scale(stream.astype(F32), post_gain[0]).astype(BF16)

    def mine(array):
        row = lax.dynamic_slice_in_dim(array, ix, 1, 0).reshape(X, C, width // (X * C))
        return lax.dynamic_slice_in_dim(row, ic, 1, 1).reshape(1, width // C)

    batch = spread(mine(normed_two), ("y", "z"), Y * Z).reshape(Y * Z, width // C)
    gate_up = gate_up.transpose(1, 0, 2).reshape(gate_up.shape[1], width // C)
    part = lax.dot_general(batch, gate_up, (((1,), (1,)), ((), ())), preferred_element_type=F32)
    both = jnp.sum(lax.all_gather(part, "c", axis=0), axis=0)
    units = w_gate.shape[2]
    hidden = (jax.nn.silu(both[:, :units]) * both[:, units:]).astype(BF16)
    down = down.transpose(1, 0, 2).reshape(units, width // C)
    part = jnp.dot(hidden, down, preferred_element_type=F32).astype(BF16)
    lowered = jnp.sum(swap(part.reshape(Y * Z, 1, width // C), ("y", "z")).astype(F32), axis=0)
    piece = (mine(stream).astype(F32) + lowered).astype(BF16)
    piece = spread(piece, ("y", "z"), Y * Z).reshape(Y * Z, width // C)
    piece = spread(piece, "x", X).reshape(X * Y * Z, width // C)
    whole = lax.all_gather(piece, "c", axis=0)
    mean_square = jnp.sum(jnp.square(whole.astype(F32)), axis=(0, 2)) / width
    gain = final_gain.reshape(X, C, width // (X * C)).transpose(1, 0, 2).reshape(C, 1, width // C)
    final = (whole.astype(F32) * lax.rsqrt(mean_square + EPSILON)[None, :, None] * gain).astype(
        BF16
    )
    vocab = w_vocab.reshape(X, C, width // (X * C), w_vocab.shape[1]).transpose(1, 0, 2, 3)
    vocab = vocab.reshape(C, width // C, w_vocab.shape[1])
    logits = jnp.dot(final[0], vocab[0], preferred_element_type=F32)
    logits = logits + jnp.dot(final[1], vocab[1], preferred_element_type=F32)
    logits = logits.astype(BF16).reshape(X, Y * Z, w_vocab.shape[1]).transpose(1, 0, 2)
    return logits.reshape(X * Y * Z, w_vocab.shape[1])


def solution(mesh):
    fine = Mesh(mesh.devices.reshape(Y, Z, X, C), ("y", "z", "x", "c"))
    req, head = (("y", "z"), ("x", "c"))
    in_specs = (
        P(req, None),
        P(),
        P(None, None, req, head, None),
        P(None, req, head, None),
        P(None, None, head),
        P(None, head, req),
        P(),
        P(),
        P(),
        P(),
        P(None, head, req),
        P(None, head, req),
        P(None, req, head),
        P(),
        P(None, req + head),
    )
    out_specs = P(None, req + head)
    return jax.shard_map(local, mesh=fine, in_specs=in_specs, out_specs=out_specs, check_vma=False)
```

profile of v0, /device:TPU:1, one launch (start us, length us, event | category | flops | bytes accessed | tf_op | source)
XLA Modules:
  0.0 240.8 jit_solution(1843471291022749129)
XLA Ops:
  6.5 0.9 fusion.26
  7.5 0.8 fusion.28
  8.5 0.6 copy.39
  9.1 15.7 %all-to-all-start = ((bf16[16,4,128]{2,1,0:T(4,128)(2,1)}), bf16[16,4,128]{2,1,0:T(4,128)(2,1)S(1)}, u32[]{:S(2)}, u32[]{:S(2)}) async-start(bf16[16,4,128]{2,1,0:T(4,128)(2,1)} %copy.39), calls=%async_computation | async-start | bytes 32768 | tf_op jit(solution)/shard_map/all_to_all | solution.py:25
  24.9 27.0 %all_gather.28 = bf16[512,256]{1,0:T(8,128)(2,1)} all-gather(bf16[32,256]{1,0:T(8,128)(2,1)} %bitcast.114), channel_id=1, replica_groups=mesh['y'=4,'z'=16,'x'=4,'c'=2] {'z'}, dimensions={0}, use_global_device_ids=true | all-gather | bytes 278528 | tf_op jit(solution)/shard_map/all_gather | solution.py:55
  52.0 0.8 dynamic-slice_bitcast_fusion
  52.7 0.2 reduce-window.8
  52.9 0.8 dynamic-slice_convert_fusion.1
  53.8 10.2 %all-gather = bf16[1,128,1,512]{3,1,2,0:T(8,128)(2,1)S(1)} all-gather(bf16[1,32,1,512]{3,1,2,0:T(8,128)(2,1)} %param.18), channel_id=2, replica_groups=mesh['y'=4,'z'=16,'x'=4,'c'=2] {'y'}, dimensions={1}, use_global_device_ids=true | all-gather | bytes 163840 | tf_op jit(solution)/shard_map/all_gather | solution.py:54
  64.0 0.1 convolution_convert_fusion.1
  64.1 0.7 reshape.262
  64.8 7.5 %all-to-all-start.1 = ((bf16[16,4,512]{2,1,0:T(4,128)(2,1)}), bf16[16,4,512]{2,1,0:T(4,128)(2,1)S(1)}, u32[]{:S(2)}, u32[]{:S(2)}) async-start(bf16[16,4,512]{2,1,0:T(4,128)(2,1)} %reshape.262), calls=%async_computation.1 | async-start | bytes 131072 | tf_op jit(solution)/shard_map/all_to_all | solution.py:25
  72.5 11.4 %all-to-all-done.1 = bf16[16,4,512]{2,1,0:T(4,128)(2,1)S(1)} async-done(((bf16[16,4,512]{2,1,0:T(4,128)(2,1)}), bf16[16,4,512]{2,1,0:T(4,128)(2,1)S(1)}, u32[]{:S(2)}, u32[]{:S(2)}) %all-to-all-start.1) | async-done | bytes 65568 | tf_op jit(solution)/shard_map/all_to_all | solution.py:25
  84.6 0.2 multiply_reduce_fusion.1
  84.8 0.3 fusion.50
  85.1 2.8 %all-gather.6.cloned.1.call-done = bf16[2048,256]{1,0:T(8,128)(2,1)} async-done(((bf16[512,256]{1,0:T(8,128)(2,1)}), bf16[2048,256]{1,0:T(8,128)(2,1)}) %all-gather.6.cloned.1.call-update) | async-done | bytes 1048592 | tf_op jit(solution)/shard_map/all_gather | solution.py:56
  87.9 1.7 fusion.14
  89.6 0.7 broadcast_in_dim.26
  90.4 14.3 %all-to-all-start.2 = ((f32[8,4,2048]{2,1,0:T(4,128)}), f32[8,4,2048]{2,1,0:T(4,128)S(1)}, u32[]{:S(2)}, u32[]{:S(2)}) async-start(f32[8,4,2048]{2,1,0:T(4,128)} %broadcast_in_dim.26), calls=%async_computation.2 | async-start | bytes 524288 | tf_op jit(solution)/shard_map/all_to_all | solution.py:25
  104.6 6.5 %all-to-all-done.2 = f32[8,4,2048]{2,1,0:T(4,128)S(1)} async-done(((f32[8,4,2048]{2,1,0:T(4,128)}), f32[8,4,2048]{2,1,0:T(4,128)S(1)}, u32[]{:S(2)}, u32[]{:S(2)}) %all-to-all-start.2) | async-done | bytes 262176 | tf_op jit(solution)/shard_map/all_to_all | solution.py:25
  111.3 0.6 dynamic-slice
  111.9 0.7 convert_reduce_fusion.2
  112.7 0.1 broadcast_in_dim.28
  112.9 0.6 broadcast.166
  113.4 1.4 reduce.7
  114.9 0.7 reshape.284
  115.6 6.1 %all-to-all-start.3 = ((bf16[64,2,512]{2,1,0:T(2,128)(2,1)}), bf16[64,2,512]{2,1,0:T(2,128)(2,1)S(1)}, u32[]{:S(2)}, u32[]{:S(2)}) async-start(bf16[64,2,512]{2,1,0:T(2,128)(2,1)} %reshape.284), calls=%async_computation.3 | async-start | bytes 262144 | tf_op jit(solution)/shard_map/all_to_all | solution.py:25
  121.7 9.8 %all_gather.34 = bf16[4,96,256]{2,1,0:T(8,128)(2,1)S(1)} all-gather(bf16[1,96,256]{2,1,0:T(8,128)(2,1)S(1)} %copy-done.6), channel_id=1, replica_groups=mesh['y'=4,'z'=16,'x'=4,'c'=2] {'x'}, dimensions={0}, use_global_device_ids=true | all-gather | bytes 245760 | tf_op jit(solution)/shard_map/all_gather | solution.py:59
  131.6 9.9 %all-gather.1 = bf16[768,256]{1,0:T(8,128)(2,1)S(1)} all-gather(bf16[192,256]{1,0:T(8,128)(2,1)S(1)} %pad_maximum_fusion), channel_id=3, replica_groups=mesh['y'=4,'z'=16,'x'=4,'c'=2] {'x'}, dimensions={0}, use_global_device_ids=true | all-gather | bytes 491520 | tf_op jit(solution)/shard_map/all_gather | solution.py:58
  141.6 0.3 copy.41
  142.0 0.3 fusion.22
  142.3 7.9 %all-gather.2 = f32[128,192]{1,0:T(8,128)S(1)} all-gather(f32[64,192]{1,0:T(8,128)S(1)} %fusion.22), channel_id=4, replica_groups=mesh['y'=4,'z'=16,'x'=4,'c'=2] {'c'}, dimensions={0}, use_global_device_ids=true | all-gather | bytes 147456 | tf_op jit(solution)/shard_map/all_gather | solution.py:104
  150.2 0.2 fusion.4
  150.4 0.7 reduce.8
  151.2 0.7 reshape.286
  151.9 15.1 %all-to-all-start.4 = ((bf16[64,2,512]{2,1,0:T(2,128)(2,1)}), bf16[64,2,512]{2,1,0:T(2,128)(2,1)S(1)}, u32[]{:S(2)}, u32[]{:S(2)}) async-start(bf16[64,2,512]{2,1,0:T(2,128)(2,1)} %reshape.286), calls=%async_computation.4 | async-start | bytes 262144 | tf_op jit(solution)/shard_map/all_to_all | solution.py:25
  167.1 14.4 %all-to-all-done.4 = bf16[64,2,512]{2,1,0:T(2,128)(2,1)S(1)} async-done(((bf16[64,2,512]{2,1,0:T(2,128)(2,1)}), bf16[64,2,512]{2,1,0:T(2,128)(2,1)S(1)}, u32[]{:S(2)}, u32[]{:S(2)}) %all-to-all-start.4) | async-done | bytes 131104 | tf_op jit(solution)/shard_map/all_to_all | solution.py:25
  181.6 0.3 convert_reduce_fusion
  181.9 0.1 broadcast_in_dim.29
  182.0 1.4 reduce.9
  183.5 21.1 %all_to_all.35 = bf16[64,2,512]{2,1,0:T(2,128)(2,1)S(1)} all-to-all(bf16[64,2,512]{2,1,0:T(2,128)(2,1)S(1)} %reshape.288), channel_id=1, replica_groups=mesh['y'=4,'z'=16,'x'=4,'c'=2] {'y','z'}, dimensions={0} | all-to-all | bytes 262144 | tf_op jit(solution)/shard_map/all_to_all | solution.py:25
  204.9 10.1 %all_to_all.36 = bf16[4,64,1024]{2,1,0:T(8,128)(2,1)} all-to-all(bf16[4,64,1024]{2,1,0:T(8,128)(2,1)S(1)} %broadcast_in_dim.31), channel_id=1, replica_groups=mesh['y'=4,'z'=16,'x'=4,'c'=2] {'x'}, dimensions={0} | all-to-all | bytes 1048576 | tf_op jit(solution)/shard_map/all_to_all | solution.py:25
  215.2 15.4 %all-gather.8.cloned.1.call-done = bf16[2,256,1024]{2,1,0:T(8,128)(2,1)} async-done(((bf16[1,256,1024]{2,1,0:T(8,128)(2,1)}), bf16[2,256,1024]{2,1,0:T(8,128)(2,1)}) %all-gather.8.cloned.1.call-update) | async-done | bytes 1048592 | tf_op jit(solution)/shard_map/all_gather | solution.py:113
  230.6 1.6 fusion
  232.2 0.3 fusion.2
  232.5 0.3 fusion.15
  232.9 0.3 fusion.3
  233.3 0.7 reshape.274
  (73 shorter events, 2.4 us)
Async XLA Ops:
  6.5 65.8 %copy-start = (bf16[1,2048,2]{1,2,0:T(2,128)(2,1)S(1)}, bf16[1,2048,2]{1,2,0:T(2,128)(2,1)}, u32[]{:S(2)}) copy-start(bf16[1,2048,2]{1,2,0:T(2,128)(2,1)} %param.19) | copy-start | bytes 24580
  6.5 77.6 %copy-start.9 = (f32[1,128]{1,0:T(1,128)S(1)}, f32[1,128]{1,0:T(1,128)}, u32[]{:S(2)}) copy-start(f32[1,128]{1,0:T(1,128)} %param.23) | copy-start | bytes 1540
  6.5 77.9 %copy-start.10 = (f32[1,128]{1,0:T(1,128)S(1)}, f32[1,128]{1,0:T(1,128)}, u32[]{:S(2)}) copy-start(f32[1,128]{1,0:T(1,128)} %param.22) | copy-start | bytes 1540
  6.5 78.2 %copy-start.11 = (bf16[1,2,1024,1,128]{4,2,3,1,0:T(8,128)(2,1)S(1)}, bf16[1,2,1024,1,128]{4,2,3,1,0:T(8,128)(2,1)}, u32[]{:S(2)}) copy-start(bf16[1,2,1024,1,128]{4,2,3,1,0:T(8,128)(2,1)} %param.17) | copy-start | bytes 1572868
  9.1 54.8 %all-to-all-start = ((bf16[16,4,128]{2,1,0:T(4,128)(2,1)}), bf16[16,4,128]{2,1,0:T(4,128)(2,1)S(1)}, u32[]{:S(2)}, u32[]{:S(2)}) async-start(bf16[16,4,128]{2,1,0:T(4,128)(2,1)} %copy.39), calls=%async_computation | async-start | bytes 32768 | tf_op jit(solution)/shard_map/all_to_all | solution.py:25
  24.9 63.0 %all-gather.6.cloned.1.call-start = ((), (), s32[]{:S(2)}) async-start(), calls=%async_computation.7 | async-start | bytes 1310720 | tf_op jit(solution)/shard_map/all_gather | solution.py:56
  64.8 19.1 %all-to-all-start.1 = ((bf16[16,4,512]{2,1,0:T(4,128)(2,1)}), bf16[16,4,512]{2,1,0:T(4,128)(2,1)S(1)}, u32[]{:S(2)}, u32[]{:S(2)}) async-start(bf16[16,4,512]{2,1,0:T(4,128)(2,1)} %reshape.262), calls=%async_computation.1 | async-start | bytes 131072 | tf_op jit(solution)/shard_map/all_to_all | solution.py:25
  87.9 23.3 %copy-start.3 = (bf16[4,2048]{1,0:T(4,128)(2,1)S(1)}, bf16[4,2048]{1,0:T(4,128)(2,1)}, u32[]{:S(2)}) copy-start(bf16[4,2048]{1,0:T(4,128)(2,1)} %param.15) | copy-start | bytes 49156
  87.9 24.0 %copy-start.8 = (f32[1,2048]{1,0:T(1,128)S(1)}, f32[1,2048]{1,0:T(1,128)}, u32[]{:S(2)}) copy-start(f32[1,2048]{1,0:T(1,128)} %param.24) | copy-start | bytes 24580
  90.4 31.4 %copy-start.6 = (bf16[1,96,256]{2,1,0:T(8,128)(2,1)S(1)}, bf16[1,96,256]{2,1,0:T(8,128)(2,1)}, u32[]{:S(2)}) copy-start(bf16[1,96,256]{2,1,0:T(8,128)(2,1)} %param.27) | copy-start | bytes 147460
  90.4 20.8 %all-to-all-start.2 = ((f32[8,4,2048]{2,1,0:T(4,128)}), f32[8,4,2048]{2,1,0:T(4,128)S(1)}, u32[]{:S(2)}, u32[]{:S(2)}) async-start(f32[8,4,2048]{2,1,0:T(4,128)} %broadcast_in_dim.26), calls=%async_computation.2 | async-start | bytes 524288 | tf_op jit(solution)/shard_map/all_to_all | solution.py:25
  111.2 20.4 %copy-start.4 = (bf16[1,256,96]{1,2,0:T(8,128)(2,1)S(1)}, bf16[1,256,96]{1,2,0:T(8,128)(2,1)}, u32[]{:S(2)}) copy-start(bf16[1,256,96]{1,2,0:T(8,128)(2,1)} %param.26) | copy-start | bytes 147460
  111.2 20.4 %copy-start.5 = (bf16[1,256,96]{1,2,0:T(8,128)(2,1)S(1)}, bf16[1,256,96]{1,2,0:T(8,128)(2,1)}, u32[]{:S(2)}) copy-start(bf16[1,256,96]{1,2,0:T(8,128)(2,1)} %param.25) | copy-start | bytes 147460
  115.6 26.3 %all-to-all-start.3 = ((bf16[64,2,512]{2,1,0:T(2,128)(2,1)}), bf16[64,2,512]{2,1,0:T(2,128)(2,1)S(1)}, u32[]{:S(2)}, u32[]{:S(2)}) async-start(bf16[64,2,512]{2,1,0:T(2,128)(2,1)} %reshape.284), calls=%async_computation.3 | async-start | bytes 262144 | tf_op jit(solution)/shard_map/all_to_all | solution.py:25
  151.9 29.6 %all-to-all-start.4 = ((bf16[64,2,512]{2,1,0:T(2,128)(2,1)}), bf16[64,2,512]{2,1,0:T(2,128)(2,1)S(1)}, u32[]{:S(2)}, u32[]{:S(2)}) async-start(bf16[64,2,512]{2,1,0:T(2,128)(2,1)} %reshape.286), calls=%async_computation.4 | async-start | bytes 262144 | tf_op jit(solution)/shard_map/all_to_all | solution.py:25
  167.1 63.6 %all-gather.8.cloned.1.call-start = ((), (), s32[]{:S(2)}) async-start(), calls=%async_computation.8 | async-start | bytes 1572864 | tf_op jit(solution)/shard_map/all_gather | solution.py:113
  204.8 10.3 %copy-start.7 = (f32[2048]{0:T(1024)S(1)}, f32[2048]{0:T(1024)}, u32[]{:S(2)}) copy-start(f32[2048]{0:T(1024)} %param.28) | copy-start | bytes 24580
  204.8 10.3 %copy-start.2 = (bf16[2048,256]{1,0:T(8,128)(2,1)S(1)}, bf16[2048,256]{1,0:T(8,128)(2,1)}, u32[]{:S(2)}) copy-start(bf16[2048,256]{1,0:T(8,128)(2,1)} %param.29) | copy-start | bytes 3145732
  230.6 1.6 copy-start.1
Sparse Core Ops, SparseCore 0:
  52.1 35.7 all-gather.5
  215.2 15.3 all-gather.7
where the time goes:
time: 242 us; the launch traced here: 241 us
  blocking collectives  96.2 us (40%)
  starting transfers between devices  58.9 us (24%)
  waiting for transfers between devices  50.5 us (21%)
  between operations  13.8 us (6%)
  other arithmetic  10.3 us (4%)
  local copies, waits for them, and re-layouts  7.77 us (3%)
  matrix products  3.4 us (1%)
    all_to_all x5, starting transfers between devices, swap(): return lax.all_to_all(values, axes, split_axis=0, concat_axis=0, tiled=True)  58.8 us
    all_to_all x5, waiting for transfers between devices, swap(): return lax.all_to_all(values, axes, split_axis=0, concat_axis=0, tiled=True)  32.3 us
    all_to_all x2, blocking collectives, swap(): return lax.all_to_all(values, axes, split_axis=0, concat_axis=0, tiled=True)  31.3 us
    all_gather x1, blocking collectives, local(): out_part = lax.all_gather(w_out[0].T, 'z', axis=0, tiled=True)  27 us
    all_gather x1, waiting for transfers between devices, local(): whole = lax.all_gather(piece, 'c', axis=0)  15.4 us
    all_gather x1, blocking collectives, local(): qkv_block = lax.all_gather(w_qkv[0, :, 0], 'y', axis=0, tiled=True)  10.2 us
    all_gather x1, blocking collectives, local(): gate_up = lax.all_gather(gate_up, 'x', axis=0)  9.93 us
    all_gather x1, blocking collectives, local(): down = lax.all_gather(w_down[0], 'x', axis=0)  9.83 us
  transfers between devices with their start and end apart: 7, of which 5 were waited for; matrix products, arithmetic and copies ran while one was open for 2% of the time, Pallas kernels for 0%

commit v1 on v0

--- a/solution.py
+++ b/solution.py
@@ -52,7 +52,9 @@
     req = lax.axis_index(("y", "z"))
     ix, ic = (lax.axis_index("x"), lax.axis_index("c"))
     qkv_block = lax.all_gather(w_qkv[0, :, 0], "y", axis=0, tiled=True)
-    out_part = lax.all_gather(w_out[0].T, "z", axis=0, tiled=True)
+    out_part = jnp.concatenate(
+        lax.all_to_all(jnp.stack([w_out[0].T] * lax.axis_size("z")), "z", 0, 0), axis=0
+    )
     out_block = lax.all_gather(out_part, "y", axis=0, tiled=True)
     gate_up = jnp.concatenate([w_gate[0].T, w_up[0].T], axis=0)
     gate_up = lax.all_gather(gate_up, "x", axis=0)

time: 242 us -> 264 us (1.091)
  waiting for transfers between devices: 50.5 us -> 90.9 us
  blocking collectives: 96.2 us -> 69.6 us
  starting transfers between devices: 58.9 us -> 65.4 us
    all_gather x1, waiting for transfers between devices: 2.8 us -> 30.9 us  [local(): out_block = lax.all_gather(out_part, 'y', axis=0, tiled=True)]
    all_gather x1 -> x0, blocking collectives: 27 us -> none  [local(): out_part = lax.all_gather(w_out[0].T, 'z', axis=0, tiled=True)]
    all_to_all x0 -> x1, waiting for transfers between devices: none -> 12.3 us  [local(): lax.all_to_all(jnp.stack([w_out[0].T] * lax.axis_size('z')), 'z', 0, 0)]
    all_to_all x0 -> x1, starting transfers between devices: none -> 3.53 us  [local(): lax.all_to_all(jnp.stack([w_out[0].T] * lax.axis_size('z')), 'z', 0, 0)]
    all_to_all x5, starting transfers between devices: 58.8 us -> 61.8 us  [swap(): return lax.all_to_all(values, axes, split_axis=0, concat_axis=0, tiled=True)]
  transfers between devices with their start and end apart: 7 -> 8, of which waited for: 5 -> 6; matrix products, arithmetic and copies ran while one was open for 2% -> 1% of each run, Pallas kernels for 0% -> 0%
where the time goes in v1:
time: 264 us; the launch traced here: 263 us
  waiting for transfers between devices  90.9 us (34%)
  blocking collectives  69.6 us (26%)
  starting transfers between devices  65.4 us (25%)
  between operations  13.8 us (5%)
  other arithmetic  10.3 us (4%)
  local copies, waits for them, and re-layouts  9.21 us (3%)
  matrix products  3.4 us (1%)
    all_to_all x5, starting transfers between devices, swap(): return lax.all_to_all(values, axes, split_axis=0, concat_axis=0, tiled=True)  61.8 us
    all_to_all x5, waiting for transfers between devices, swap(): return lax.all_to_all(values, axes, split_axis=0, concat_axis=0, tiled=True)  32.3 us
    all_to_all x2, blocking collectives, swap(): return lax.all_to_all(values, axes, split_axis=0, concat_axis=0, tiled=True)  31.3 us
    all_gather x1, waiting for transfers between devices, local(): out_block = lax.all_gather(out_part, 'y', axis=0, tiled=True)  30.9 us
    all_gather x1, waiting for transfers between devices, local(): whole = lax.all_gather(piece, 'c', axis=0)  15.4 us
    all_to_all x1, waiting for transfers between devices, local(): lax.all_to_all(jnp.stack([w_out[0].T] * lax.axis_size('z')), 'z', 0, 0)  12.3 us
    all_gather x1, blocking collectives, local(): qkv_block = lax.all_gather(w_qkv[0, :, 0], 'y', axis=0, tiled=True)  10.7 us
    all_gather x1, blocking collectives, local(): gate_up = lax.all_gather(gate_up, 'x', axis=0)  9.93 us
  transfers between devices with their start and end apart: 8, of which 6 were waited for; matrix products, arithmetic and copies ran while one was open for 1% of the time, Pallas kernels for 0%

profile of v1, /device:TPU:1, one launch (start us, length us, event | category | flops | bytes accessed | tf_op | source)
XLA Modules:
  0.0 262.7 jit_solution(6641081564966816011)
XLA Ops:
  6.5 0.9 fusion.26
  7.4 0.8 fusion.28
  8.5 0.6 copy.39
  9.1 15.7 %all-to-all-start = ((bf16[16,4,128]{2,1,0:T(4,128)(2,1)}), bf16[16,4,128]{2,1,0:T(4,128)(2,1)S(1)}, u32[]{:S(2)}, u32[]{:S(2)}) async-start(bf16[16,4,128]{2,1,0:T(4,128)(2,1)} %copy.39), calls=%async_computation | async-start | bytes 32768 | tf_op jit(solution)/shard_map/all_to_all | solution.py:25
  24.9 0.8 dynamic-slice_bitcast_fusion
  25.7 0.2 reduce-window.8
  25.8 0.8 dynamic-slice_convert_fusion.1
  26.7 10.7 %all-gather = bf16[1,128,1,512]{3,1,2,0:T(8,128)(2,1)S(1)} all-gather(bf16[1,32,1,512]{3,1,2,0:T(8,128)(2,1)} %param.18), channel_id=2, replica_groups=mesh['y'=4,'z'=16,'x'=4,'c'=2] {'y'}, dimensions={1}, use_global_device_ids=true | all-gather | bytes 163840 | tf_op jit(solution)/shard_map/all_gather | solution.py:54
  37.5 0.7 reshape.267
  38.2 10.6 %all-to-all-start.1 = ((bf16[16,4,512]{2,1,0:T(4,128)(2,1)}), bf16[16,4,512]{2,1,0:T(4,128)(2,1)S(1)}, u32[]{:S(2)}, u32[]{:S(2)}) async-start(bf16[16,4,512]{2,1,0:T(4,128)(2,1)} %reshape.267), calls=%async_computation.1 | async-start | bytes 131072 | tf_op jit(solution)/shard_map/all_to_all | solution.py:25
  48.9 11.4 %all-to-all-done.1 = bf16[16,4,512]{2,1,0:T(4,128)(2,1)S(1)} async-done(((bf16[16,4,512]{2,1,0:T(4,128)(2,1)}), bf16[16,4,512]{2,1,0:T(4,128)(2,1)S(1)}, u32[]{:S(2)}, u32[]{:S(2)}) %all-to-all-start.1) | async-done | bytes 65568 | tf_op jit(solution)/shard_map/all_to_all | solution.py:25
  60.3 0.7 stack.2
  61.1 3.5 %all-to-all-start.2 = ((bf16[16,32,256]{2,1,0:T(8,128)(2,1)}), bf16[16,32,256]{2,1,0:T(8,128)(2,1)S(1)}, u32[]{:S(2)}, u32[]{:S(2)}) async-start(bf16[16,32,256]{2,1,0:T(8,128)(2,1)} %stack.2), calls=%async_computation.2 | async-start | bytes 524288 | tf_op jit(solution)/shard_map/all_to_all | solution.py:56
  65.1 12.3 %all-to-all-done.2 = bf16[16,32,256]{2,1,0:T(8,128)(2,1)S(1)} async-done(((bf16[16,32,256]{2,1,0:T(8,128)(2,1)}), bf16[16,32,256]{2,1,0:T(8,128)(2,1)S(1)}, u32[]{:S(2)}, u32[]{:S(2)}) %all-to-all-start.2) | async-done | bytes 262176 | tf_op jit(solution)/shard_map/all_to_all | solution.py:56
  77.4 0.7 copy-done.3
  78.4 0.2 multiply_reduce_fusion.1
  78.5 0.3 fusion.50
  78.9 30.9 %all-gather.6.cloned.1.call-done = bf16[2048,256]{1,0:T(8,128)(2,1)} async-done(((bf16[512,256]{1,0:T(8,128)(2,1)}), bf16[2048,256]{1,0:T(8,128)(2,1)}) %all-gather.6.cloned.1.call-update) | async-done | bytes 1048592 | tf_op jit(solution)/shard_map/all_gather | solution.py:58
  109.8 1.7 fusion.14
  111.5 0.7 broadcast_in_dim.26
  112.2 6.0 %all-to-all-start.3 = ((f32[8,4,2048]{2,1,0:T(4,128)}), f32[8,4,2048]{2,1,0:T(4,128)S(1)}, u32[]{:S(2)}, u32[]{:S(2)}) async-start(f32[8,4,2048]{2,1,0:T(4,128)} %broadcast_in_dim.26), calls=%async_computation.3 | async-start | bytes 524288 | tf_op jit(solution)/shard_map/all_to_all | solution.py:25
  118.2 6.5 %all-to-all-done.3 = f32[8,4,2048]{2,1,0:T(4,128)S(1)} async-done(((f32[8,4,2048]{2,1,0:T(4,128)}), f32[8,4,2048]{2,1,0:T(4,128)S(1)}, u32[]{:S(2)}, u32[]{:S(2)}) %all-to-all-start.3) | async-done | bytes 262176 | tf_op jit(solution)/shard_map/all_to_all | solution.py:25
  124.9 0.6 dynamic-slice
  125.5 0.7 convert_reduce_fusion.2
  126.4 0.6 broadcast.168
  127.0 1.4 reduce.7
  128.5 0.7 reshape.290
  129.2 14.4 %all-to-all-start.4 = ((bf16[64,2,512]{2,1,0:T(2,128)(2,1)}), bf16[64,2,512]{2,1,0:T(2,128)(2,1)S(1)}, u32[]{:S(2)}, u32[]{:S(2)}) async-start(bf16[64,2,512]{2,1,0:T(2,128)(2,1)} %reshape.290), calls=%async_computation.4 | async-start | bytes 262144 | tf_op jit(solution)/shard_map/all_to_all | solution.py:25
  143.6 9.8 %all_gather.30 = bf16[4,96,256]{2,1,0:T(8,128)(2,1)S(1)} all-gather(bf16[1,96,256]{2,1,0:T(8,128)(2,1)S(1)} %copy-done.7), channel_id=1, replica_groups=mesh['y'=4,'z'=16,'x'=4,'c'=2] {'x'}, dimensions={0}, use_global_device_ids=true | all-gather | bytes 245760 | tf_op jit(solution)/shard_map/all_gather | solution.py:61
  153.5 9.9 %all-gather.1 = bf16[768,256]{1,0:T(8,128)(2,1)S(1)} all-gather(bf16[192,256]{1,0:T(8,128)(2,1)S(1)} %pad_maximum_fusion), channel_id=3, replica_groups=mesh['y'=4,'z'=16,'x'=4,'c'=2] {'x'}, dimensions={0}, use_global_device_ids=true | all-gather | bytes 491520 | tf_op jit(solution)/shard_map/all_gather | solution.py:60
  163.4 0.3 copy.41
  163.9 0.3 fusion.22
  164.2 7.9 %all-gather.2 = f32[128,192]{1,0:T(8,128)S(1)} all-gather(f32[64,192]{1,0:T(8,128)S(1)} %fusion.22), channel_id=4, replica_groups=mesh['y'=4,'z'=16,'x'=4,'c'=2] {'c'}, dimensions={0}, use_global_device_ids=true | all-gather | bytes 147456 | tf_op jit(solution)/shard_map/all_gather | solution.py:106
  172.1 0.2 fusion.4
  172.3 0.7 reduce.8
  173.1 0.7 reshape.292
  173.8 15.1 %all-to-all-start.5 = ((bf16[64,2,512]{2,1,0:T(2,128)(2,1)}), bf16[64,2,512]{2,1,0:T(2,128)(2,1)S(1)}, u32[]{:S(2)}, u32[]{:S(2)}) async-start(bf16[64,2,512]{2,1,0:T(2,128)(2,1)} %reshape.292), calls=%async_computation.5 | async-start | bytes 262144 | tf_op jit(solution)/shard_map/all_to_all | solution.py:25
  189.0 14.4 %all-to-all-done.5 = bf16[64,2,512]{2,1,0:T(2,128)(2,1)S(1)} async-done(((bf16[64,2,512]{2,1,0:T(2,128)(2,1)}), bf16[64,2,512]{2,1,0:T(2,128)(2,1)S(1)}, u32[]{:S(2)}, u32[]{:S(2)}) %all-to-all-start.5) | async-done | bytes 131104 | tf_op jit(solution)/shard_map/all_to_all | solution.py:25
  203.5 0.3 convert_reduce_fusion
  203.9 1.4 reduce.9
  205.4 21.1 %all_to_all.40 = bf16[64,2,512]{2,1,0:T(2,128)(2,1)S(1)} all-to-all(bf16[64,2,512]{2,1,0:T(2,128)(2,1)S(1)} %reshape.294), channel_id=1, replica_groups=mesh['y'=4,'z'=16,'x'=4,'c'=2] {'y','z'}, dimensions={0} | all-to-all | bytes 262144 | tf_op jit(solution)/shard_map/all_to_all | solution.py:25
  226.8 10.1 %all_to_all.41 = bf16[4,64,1024]{2,1,0:T(8,128)(2,1)} all-to-all(bf16[4,64,1024]{2,1,0:T(8,128)(2,1)S(1)} %broadcast_in_dim.31), channel_id=1, replica_groups=mesh['y'=4,'z'=16,'x'=4,'c'=2] {'x'}, dimensions={0} | all-to-all | bytes 1048576 | tf_op jit(solution)/shard_map/all_to_all | solution.py:25
  237.1 15.4 %all-gather.8.cloned.1.call-done = bf16[2,256,1024]{2,1,0:T(8,128)(2,1)} async-done(((bf16[1,256,1024]{2,1,0:T(8,128)(2,1)}), bf16[2,256,1024]{2,1,0:T(8,128)(2,1)}) %all-gather.8.cloned.1.call-update) | async-done | bytes 1048592 | tf_op jit(solution)/shard_map/all_gather | solution.py:115
  252.5 1.6 fusion
  254.1 0.3 fusion.2
  254.4 0.3 fusion.15
  254.7 0.3 fusion.3
  255.2 0.7 reshape.280
  (79 shorter events, 2.8 us)
Async XLA Ops:
  6.5 42.2 %copy-start = (bf16[1,2048,2]{1,2,0:T(2,128)(2,1)S(1)}, bf16[1,2048,2]{1,2,0:T(2,128)(2,1)}, u32[]{:S(2)}) copy-start(bf16[1,2048,2]{1,2,0:T(2,128)(2,1)} %param.19) | copy-start | bytes 24580
  6.5 53.8 %copy-start.8 = (bf16[1,256,32]{1,2,0:T(8,128)(2,1)S(1)}, bf16[1,256,32]{1,2,0:T(8,128)(2,1)}, u32[]{:S(2)}) copy-start(bf16[1,256,32]{1,2,0:T(8,128)(2,1)} %param.20) | copy-start | bytes 49156
  6.5 58.4 %copy-start.11 = (f32[1,128]{1,0:T(1,128)S(1)}, f32[1,128]{1,0:T(1,128)}, u32[]{:S(2)}) copy-start(f32[1,128]{1,0:T(1,128)} %param.23) | copy-start | bytes 1540
  8.4 69.8 %copy-start.12 = (f32[1,128]{1,0:T(1,128)S(1)}, f32[1,128]{1,0:T(1,128)}, u32[]{:S(2)}) copy-start(f32[1,128]{1,0:T(1,128)} %param.22) | copy-start | bytes 1540
  8.4 70.1 %copy-start.13 = (bf16[1,2,1024,1,128]{4,2,3,1,0:T(8,128)(2,1)S(1)}, bf16[1,2,1024,1,128]{4,2,3,1,0:T(8,128)(2,1)}, u32[]{:S(2)}) copy-start(bf16[1,2,1024,1,128]{4,2,3,1,0:T(8,128)(2,1)} %param.17) | copy-start | bytes 1572868
  9.1 28.2 %all-to-all-start = ((bf16[16,4,128]{2,1,0:T(4,128)(2,1)}), bf16[16,4,128]{2,1,0:T(4,128)(2,1)S(1)}, u32[]{:S(2)}, u32[]{:S(2)}) async-start(bf16[16,4,128]{2,1,0:T(4,128)(2,1)} %copy.39), calls=%async_computation | async-start | bytes 32768 | tf_op jit(solution)/shard_map/all_to_all | solution.py:25
  38.2 22.2 %all-to-all-start.1 = ((bf16[16,4,512]{2,1,0:T(4,128)(2,1)}), bf16[16,4,512]{2,1,0:T(4,128)(2,1)S(1)}, u32[]{:S(2)}, u32[]{:S(2)}) async-start(bf16[16,4,512]{2,1,0:T(4,128)(2,1)} %reshape.267), calls=%async_computation.1 | async-start | bytes 131072 | tf_op jit(solution)/shard_map/all_to_all | solution.py:25
  61.1 16.3 %all-to-all-start.2 = ((bf16[16,32,256]{2,1,0:T(8,128)(2,1)}), bf16[16,32,256]{2,1,0:T(8,128)(2,1)S(1)}, u32[]{:S(2)}, u32[]{:S(2)}) async-start(bf16[16,32,256]{2,1,0:T(8,128)(2,1)} %stack.2), calls=%async_computation.2 | async-start | bytes 524288 | tf_op jit(solution)/shard_map/all_to_all | solution.py:56
  64.6 45.2 %all-gather.6.cloned.1.call-start = ((), (), s32[]{:S(2)}) async-start(), calls=%async_computation.8 | async-start | bytes 1310720 | tf_op jit(solution)/shard_map/all_gather | solution.py:58
  77.4 0.7 copy-start.3
  109.8 15.0 %copy-start.4 = (bf16[4,2048]{1,0:T(4,128)(2,1)S(1)}, bf16[4,2048]{1,0:T(4,128)(2,1)}, u32[]{:S(2)}) copy-start(bf16[4,2048]{1,0:T(4,128)(2,1)} %param.15) | copy-start | bytes 49156
  109.8 15.7 %copy-start.10 = (f32[1,2048]{1,0:T(1,128)S(1)}, f32[1,2048]{1,0:T(1,128)}, u32[]{:S(2)}) copy-start(f32[1,2048]{1,0:T(1,128)} %param.24) | copy-start | bytes 24580
  112.2 31.4 %copy-start.7 = (bf16[1,96,256]{2,1,0:T(8,128)(2,1)S(1)}, bf16[1,96,256]{2,1,0:T(8,128)(2,1)}, u32[]{:S(2)}) copy-start(bf16[1,96,256]{2,1,0:T(8,128)(2,1)} %param.27) | copy-start | bytes 147460
  112.2 12.5 %all-to-all-start.3 = ((f32[8,4,2048]{2,1,0:T(4,128)}), f32[8,4,2048]{2,1,0:T(4,128)S(1)}, u32[]{:S(2)}, u32[]{:S(2)}) async-start(f32[8,4,2048]{2,1,0:T(4,128)} %broadcast_in_dim.26), calls=%async_computation.3 | async-start | bytes 524288 | tf_op jit(solution)/shard_map/all_to_all | solution.py:25
  124.8 28.7 %copy-start.5 = (bf16[1,256,96]{1,2,0:T(8,128)(2,1)S(1)}, bf16[1,256,96]{1,2,0:T(8,128)(2,1)}, u32[]{:S(2)}) copy-start(bf16[1,256,96]{1,2,0:T(8,128)(2,1)} %param.26) | copy-start | bytes 147460
  124.8 28.7 %copy-start.6 = (bf16[1,256,96]{1,2,0:T(8,128)(2,1)S(1)}, bf16[1,256,96]{1,2,0:T(8,128)(2,1)}, u32[]{:S(2)}) copy-start(bf16[1,256,96]{1,2,0:T(8,128)(2,1)} %param.25) | copy-start | bytes 147460
  129.2 34.6 %all-to-all-start.4 = ((bf16[64,2,512]{2,1,0:T(2,128)(2,1)}), bf16[64,2,512]{2,1,0:T(2,128)(2,1)S(1)}, u32[]{:S(2)}, u32[]{:S(2)}) async-start(bf16[64,2,512]{2,1,0:T(2,128)(2,1)} %reshape.290), calls=%async_computation.4 | async-start | bytes 262144 | tf_op jit(solution)/shard_map/all_to_all | solution.py:25
  173.8 29.6 %all-to-all-start.5 = ((bf16[64,2,512]{2,1,0:T(2,128)(2,1)}), bf16[64,2,512]{2,1,0:T(2,128)(2,1)S(1)}, u32[]{:S(2)}, u32[]{:S(2)}) async-start(bf16[64,2,512]{2,1,0:T(2,128)(2,1)} %reshape.292), calls=%async_computation.5 | async-start | bytes 262144 | tf_op jit(solution)/shard_map/all_to_all | solution.py:25
  188.9 63.6 %all-gather.8.cloned.1.call-start = ((), (), s32[]{:S(2)}) async-start(), calls=%async_computation.9 | async-start | bytes 1572864 | tf_op jit(solution)/shard_map/all_gather | solution.py:115
  226.7 10.3 %copy-start.9 = (f32[2048]{0:T(1024)S(1)}, f32[2048]{0:T(1024)}, u32[]{:S(2)}) copy-start(f32[2048]{0:T(1024)} %param.28) | copy-start | bytes 24580
  226.7 10.3 %copy-start.2 = (bf16[2048,256]{1,0:T(8,128)(2,1)S(1)}, bf16[2048,256]{1,0:T(8,128)(2,1)}, u32[]{:S(2)}) copy-start(bf16[2048,256]{1,0:T(8,128)(2,1)} %param.29) | copy-start | bytes 3145732
  252.5 1.6 copy-start.1
Sparse Core Ops, SparseCore 0:
  78.2 31.4 all-gather.5
  237.1 15.3 all-gather.7
